TPU v7x, 32 devices: a whole 2x2x4 slice. The times are simulated.
32 devices in a mesh: dp: 2 (over x), seq: 16 (over z, y, core).
Axes of the slice: x: 2, y: 2, z: 4, core: 2. Of those that a mesh axis runs over, the one named last changes fastest.
Arguments:
- pixels: bfloat16 [4096, 768], P(('dp', 'seq')), may hold values from -6 to 6
- mask: int32 [4096], P(('dp', 'seq')), may hold values 0 or 1
- image_count: int32 [2, 6], P('dp'), may hold values from 1 to 1024, 2048 in all within a row
- image_width: int32 [2, 6], P('dp'), may hold values from 4 to 63
- gsd_index: int32 [2, 6], P('dp'), may hold values from 0 to 8
- step: int32 [1], replicated, may hold values from 2 to 20
- master: float32 [17551360], P(('dp', 'seq')), as said below
- moment_one: float32 [17551360], P(('dp', 'seq')), as said below
- moment_two: float32 [17551360], P(('dp', 'seq')), as said below
Outputs:
- new_master: float32 [17551360], P(('dp', 'seq'))
- new_moment_one: float32 [17551360], P(('dp', 'seq'))
- new_moment_two: float32 [17551360], P(('dp', 'seq'))
- loss: float32 [1], replicated
- grad_norm: float32 [1], replicated
Inputs may be any that keep to these rules, and one draw needn't show every extreme that they name: master holds each weight drawn by its fan-in, gains near 1. moment_two is positive. moment_one takes both signs.
All inputs are finite; a program needn't handle non-finite values. No bound on the sum of `mask` on one device may be relied on, other than what follows from the above.
Results may differ from a plain program's by a relative error of at most 0.0024.
The roundings to bfloat16 on the way count: a program that leaves them out, or rounds other values in their place, can miss the bound.
Values may be sent and summed in bfloat16 or wider, within the bound.
A program may use at most 512 MiB of HBM per device.

v0:
```python
import math
import jax
import jax.numpy as jnp
from jax import lax
from jax.sharding import PartitionSpec as P

D = 1024
HEADS = 16
FF = 4096
DD = 512
DHEADS = 16
DFF = 2048
PATCH = 16
PIX = 768
LOWPIX = 192
clip_level = 0.0001
peak_rate = 0.1
warm_steps = 10.0
decay_rate = 0.05
adam_eps = 1e-12


def param_shapes():
    return [
        (PIX, D),
        (D,),
        (4, D),
        (D, 3 * D),
        (D, D),
        (D,),
        (D, FF),
        (FF,),
        (FF, D),
        (D,),
        (D, DD),
        (DD,),
        (DD,),
        (4, DD),
        (DD, 3 * DD),
        (DD, DD),
        (DD,),
        (DD, DFF),
        (DFF,),
        (DFF, DD),
        (DD,),
        (DD, PIX),
        (PIX,),
        (DD, LOWPIX),
        (LOWPIX,),
    ]


def unpack(flat):
    pieces = []
    offset = 0
    for shape in param_shapes():
        length = math.prod(shape)
        pieces.append(lax.slice_in_dim(flat, offset, offset + length).reshape(shape))
        offset += length
    return pieces


def matmul(a, b):
    return jnp.dot(a, b, preferred_element_type=jnp.float32)


def outer(a, b):
    return lax.dot_general(a, b, (((0,), (0,)), ((), ())), preferred_element_type=jnp.float32)


def back_mul(a, weight):
    return lax.dot_general(a, weight, (((1,), (1,)), ((), ())), preferred_element_type=jnp.float32)


def layer_norm(x, gain, shift):
    centred = x - jnp.mean(x, axis=-1, keepdims=True)
    return (
        centred * lax.rsqrt(jnp.mean(centred * centred, axis=-1, keepdims=True) + 1e-06) * gain
        + shift
    )


def geometry(counts, widths, ground, places):
    ends = jnp.cumsum(counts)
    starts = ends - counts
    inside = ((places[:, None] >= starts[None, :]) & (places[:, None] < ends[None, :])).astype(
        jnp.int32
    )
    image = jnp.sum(inside * jnp.arange(counts.shape[0], dtype=jnp.int32)[None, :], axis=1)
    start = jnp.sum(inside * starts[None, :], axis=1)
    width = jnp.sum(inside * widths[None, :], axis=1)
    level = jnp.sum(inside * ground[None, :], axis=1)
    local = places - start
    row_num = local // width
    col_num = local - row_num * width
    ratio = jnp.exp2(level.astype(jnp.float32) * 0.25)
    return (image, local, row_num.astype(jnp.float32) * ratio, col_num.astype(jnp.float32) * ratio)


def position_code(row_pos, col_pos, width):
    quarter = width // 4
    freqs = jnp.power(10000.0, -jnp.arange(quarter, dtype=jnp.float32) / quarter)
    row_ang = row_pos[:, None] * freqs[None, :]
    col_ang = col_pos[:, None] * freqs[None, :]
    return jnp.concatenate(
        [jnp.sin(row_ang), jnp.cos(row_ang), jnp.sin(col_ang), jnp.cos(col_ang)], axis=1
    )


def pool_table():
    values = 3 * PATCH * PATCH
    index = jnp.arange(values, dtype=jnp.int32)
    channel = index % 3
    cell = index // 3
    row_num = cell // PATCH
    col_num = cell % PATCH
    target = (row_num // 2 * (PATCH // 2) + col_num // 2) * 3 + channel
    return (target[:, None] == jnp.arange(values // 4, dtype=jnp.int32)[None, :]).astype(
        jnp.float32
    ) * 0.25


def masked_scores(queries, keys, query_image, key_image, key_seen, scale):
    raw = jnp.einsum("rhd,khd->hrk", queries, keys, preferred_element_type=jnp.float32) * scale
    allowed = (query_image[:, None] == key_image[None, :]) & (key_seen[None, :] > 0)
    return jnp.where(allowed[None], raw, -1e30)


def attend(queries, keys, values, key_seen, query_image, key_image, scale):
    scores = masked_scores(queries, keys, query_image, key_image, key_seen, scale)
    top = jnp.max(scores, axis=-1)
    mass = jnp.sum(jnp.where(scores > -1e29, jnp.exp(scores - top[..., None]), 0.0), axis=-1)
    lse = top + jnp.log(mass)
    probs = jnp.exp(scores - lse[..., None]).astype(jnp.bfloat16)
    out = jnp.einsum("hrk,khd->rhd", probs, values, preferred_element_type=jnp.float32)
    return (out, lse)


def attend_back(queries, keys, values, key_seen, query_image, key_image, out, lse, grad_out, scale):
    rows, heads, depth = queries.shape
    dterm = jnp.transpose(jnp.sum(grad_out.astype(jnp.float32) * out, axis=-1))
    scores = masked_scores(queries, keys, query_image, key_image, key_seen, scale)
    probs = jnp.exp(scores - lse[..., None])
    dprob = jnp.einsum("rhd,khd->hrk", grad_out, values, preferred_element_type=jnp.float32)
    dscore = (probs * (dprob - dterm[..., None])).astype(jnp.bfloat16)
    probs_low = probs.astype(jnp.bfloat16)
    grad_queries = jnp.einsum("hrk,khd->rhd", dscore, keys, preferred_element_type=jnp.float32)
    count = rows * lax.axis_size("seq")
    grad_keys = (
        jnp.einsum("hrk,rhd->khd", dscore, queries, preferred_element_type=jnp.float32) * scale
    )
    grad_values = jnp.einsum(
        "hrk,rhd->khd", probs_low, grad_out, preferred_element_type=jnp.float32
    )
    grad_kv = lax.psum_scatter(
        jnp.concatenate([grad_keys.reshape(count, -1), grad_values.reshape(count, -1)], axis=1),
        "seq",
        scatter_dimension=0,
        tiled=True,
    )
    return (grad_queries * scale, grad_kv)


def block_forward(x, weights, seen, query_image, key_image, heads):
    norms, qkv_w, out_w, out_b, up_w, up_b, down_w, down_b = weights
    gains = norms.astype(jnp.float32)
    rows, width = x.shape
    depth = width // heads
    scale = depth ** (-0.5)
    normed = layer_norm(x, gains[0], gains[1]).astype(jnp.bfloat16)
    mixed = matmul(normed, qkv_w).astype(jnp.bfloat16)
    queries = mixed[:, :width].reshape(rows, heads, depth)
    all_keys, all_values, all_seen = (
        lax.all_gather(mixed[:, width : 2 * width], "seq", axis=0, tiled=True),
        lax.all_gather(mixed[:, 2 * width :], "seq", axis=0, tiled=True),
        lax.all_gather(seen, "seq", axis=0, tiled=True),
    )
    all_keys = all_keys.reshape(-1, heads, depth)
    all_values = all_values.reshape(-1, heads, depth)
    out, lse = attend(queries, all_keys, all_values, all_seen, query_image, key_image, scale)
    attended = out.reshape(rows, width).astype(jnp.bfloat16)
    resid = x + matmul(attended, out_w) + out_b.astype(jnp.float32)
    normed_two = layer_norm(resid, gains[2], gains[3]).astype(jnp.bfloat16)
    pre = matmul(normed_two, up_w) + up_b.astype(jnp.float32)
    hidden_act = jax.nn.gelu(pre, approximate=False).astype(jnp.bfloat16)
    result = resid + matmul(hidden_act, down_w) + down_b.astype(jnp.float32)
    kept = (
        x,
        normed,
        queries,
        all_keys,
        all_values,
        all_seen,
        out,
        lse,
        attended,
        resid,
        normed_two,
        pre,
        hidden_act,
    )
    return (result, kept)


def block_backward(grad, weights, kept, query_image, key_image, heads):
    norms, qkv_w, out_w, out_b, up_w, up_b, down_w, down_b = weights
    gains = norms.astype(jnp.float32)
    (
        x,
        normed,
        queries,
        all_keys,
        all_values,
        all_seen,
        out,
        lse,
        attended,
        resid,
        normed_two,
        pre,
        hidden_act,
    ) = kept
    rows, width = x.shape
    depth = width // heads
    grad_low = grad.astype(jnp.bfloat16)
    grad_down = outer(hidden_act, grad_low)
    grad_down_b = jnp.sum(grad, axis=0)
    _, gelu_back = jax.vjp(lambda value: jax.nn.gelu(value, approximate=False), pre)
    (grad_pre,) = gelu_back(back_mul(grad_low, down_w))
    pre_low = grad_pre.astype(jnp.bfloat16)
    grad_up = outer(normed_two, pre_low)
    grad_up_b = jnp.sum(grad_pre, axis=0)
    _, norm_two_back = jax.vjp(layer_norm, resid, gains[2], gains[3])
    grad_resid, grad_gain_two, grad_shift_two = norm_two_back(back_mul(pre_low, up_w))
    grad_resid = grad_resid + grad
    resid_low = grad_resid.astype(jnp.bfloat16)
    grad_out = outer(attended, resid_low)
    grad_out_b = jnp.sum(grad_resid, axis=0)
    grad_attended = back_mul(resid_low, out_w).astype(jnp.bfloat16).reshape(rows, heads, depth)
    grad_queries, grad_kv = attend_back(
        queries,
        all_keys,
        all_values,
        all_seen,
        query_image,
        key_image,
        out,
        lse,
        grad_attended,
        depth ** (-0.5),
    )
    mixed_low = jnp.concatenate([grad_queries.reshape(rows, width), grad_kv], axis=1).astype(
        jnp.bfloat16
    )
    grad_qkv = outer(normed, mixed_low)
    _, norm_one_back = jax.vjp(layer_norm, x, gains[0], gains[1])
    grad_x, grad_gain_one, grad_shift_one = norm_one_back(back_mul(mixed_low, qkv_w))
    grad_norms = jnp.stack([grad_gain_one, grad_shift_one, grad_gain_two, grad_shift_two])
    return (
        grad_x + grad_resid,
        [grad_norms, grad_qkv, grad_out, grad_out_b, grad_up, grad_up_b, grad_down, grad_down_b],
    )


def body(pixels, mask, image_count, image_width, gsd_index, step, master, moment_one, moment_two):
    flat = lax.all_gather(master.astype(jnp.bfloat16), ("dp", "seq"), axis=0, tiled=True)
    weights = unpack(flat)
    rows = pixels.shape[0]
    group_rows = rows * lax.axis_size("seq")
    places = lax.axis_index("seq") * rows + jnp.arange(rows, dtype=jnp.int32)
    counts, widths, ground = (image_count[0], image_width[0], gsd_index[0])
    query_image, local, row_pos, col_pos = geometry(counts, widths, ground, places)
    key_image = geometry(counts, widths, ground, jnp.arange(group_rows, dtype=jnp.int32))[0]
    hidden = ((mask == 1) & (local != 0)).astype(jnp.float32)
    count_local = jnp.sum(hidden)
    count = lax.psum(count_local, ("dp", "seq"))
    embedded = (
        matmul(pixels, weights[0])
        + weights[1].astype(jnp.float32)
        + position_code(row_pos, col_pos, D)
    )
    encoded, enc_kept = block_forward(
        embedded, weights[2:10], (1.0 - hidden).astype(jnp.bfloat16), query_image, key_image, HEADS
    )
    encoded_low = encoded.astype(jnp.bfloat16)
    projected = matmul(encoded_low, weights[10]) + weights[11].astype(jnp.float32)
    dec_in = jnp.where(
        hidden[:, None] > 0, weights[12].astype(jnp.float32)[None, :], projected
    ) + position_code(row_pos, col_pos, DD)
    decoded, dec_kept = block_forward(
        dec_in, weights[13:21], jnp.ones((rows,), jnp.bfloat16), query_image, key_image, DHEADS
    )
    decoded_low = decoded.astype(jnp.bfloat16)
    high = matmul(decoded_low, weights[21]) + weights[22].astype(jnp.float32)
    low_pred = matmul(decoded_low, weights[23]) + weights[24].astype(jnp.float32)
    table = pool_table()
    pix_wide = pixels.astype(jnp.float32)
    low_target = jnp.dot(
        pix_wide, table, precision=lax.Precision.HIGHEST, preferred_element_type=jnp.float32
    )
    high_target = pix_wide - jnp.dot(
        low_target,
        4.0 * table.T,
        precision=lax.Precision.HIGHEST,
        preferred_element_type=jnp.float32,
    )
    per_patch = jnp.mean(jnp.abs(high - high_target), axis=-1) + jnp.mean(
        (low_pred - low_target) ** 2, axis=-1
    )
    loss_local = jnp.sum(hidden * per_patch)
    grad_high = hidden[:, None] * jnp.sign(high - high_target) / PIX
    grad_low_pred = hidden[:, None] * 2.0 * (low_pred - low_target) / LOWPIX
    high_low = grad_high.astype(jnp.bfloat16)
    lowband_low = grad_low_pred.astype(jnp.bfloat16)
    grad_decoded = back_mul(high_low, weights[21]) + back_mul(lowband_low, weights[23])
    grad_dec_in, dec_grads = block_backward(
        grad_decoded, weights[13:21], dec_kept, query_image, key_image, DHEADS
    )
    grad_token = jnp.sum(hidden[:, None] * grad_dec_in, axis=0)
    grad_projected = grad_dec_in * (1.0 - hidden)[:, None]
    projected_low = grad_projected.astype(jnp.bfloat16)
    grad_encoded = back_mul(projected_low, weights[10])
    grad_embedded, enc_grads = block_backward(
        grad_encoded, weights[2:10], enc_kept, query_image, key_image, HEADS
    )
    grads = (
        [outer(pixels, grad_embedded.astype(jnp.bfloat16)), jnp.sum(grad_embedded, axis=0)]
        + enc_grads
        + [outer(encoded_low, projected_low), jnp.sum(grad_projected, axis=0), grad_token]
        + dec_grads
        + [
            outer(decoded_low, high_low),
            jnp.sum(grad_high, axis=0),
            outer(decoded_low, lowband_low),
            jnp.sum(grad_low_pred, axis=0),
        ]
    )
    shard = master.shape[0]
    groups, seqs = (lax.axis_size("dp"), lax.axis_size("seq"))
    total_params = shard * groups * seqs
    used = sum((math.prod(shape) for shape in param_shapes()))
    grad_flat = jnp.concatenate(
        [g.reshape(-1) for g in grads] + [jnp.zeros((total_params - used,), jnp.float32)]
    )
    partial_share = lax.psum_scatter(
        grad_flat.reshape(groups, seqs, shard), "seq", scatter_dimension=1, tiled=True
    )
    summed = lax.psum(partial_share, "dp")
    owned = lax.dynamic_index_in_dim(summed, lax.axis_index("dp"), 0, keepdims=False)[0]
    square_sum = jnp.sum(owned * owned)
    loss_total, square_total = lax.psum((loss_local, square_sum), ("dp", "seq"))
    grad_norm = jnp.sqrt(square_total) / count
    clipped = owned * (jnp.minimum(1.0, clip_level / grad_norm) / count)
    first = 0.5 * moment_one + 0.5 * clipped
    second = 0.5 * moment_two + 0.5 * clipped * clipped
    step_value = step[0].astype(jnp.float32)
    correction = 1.0 - jnp.power(0.5, step_value)
    rate = peak_rate * jnp.minimum(1.0, step_value / warm_steps)
    new_master = master - rate * (
        first / correction / (jnp.sqrt(second / correction) + adam_eps) + decay_rate * master
    )
    return (new_master, first, second, (loss_total / count).reshape(1), grad_norm.reshape(1))


def solution(mesh):
    in_specs = (
        P(("dp", "seq"), None),
        P(("dp", "seq")),
        P("dp", None),
        P("dp", None),
        P("dp", None),
        P(),
        P(("dp", "seq")),
        P(("dp", "seq")),
        P(("dp", "seq")),
    )
    out_specs = (P(("dp", "seq")), P(("dp", "seq")), P(("dp", "seq")), P(), P())
    return jax.shard_map(body, mesh=mesh, in_specs=in_specs, out_specs=out_specs, check_vma=False)
```

profile of v0, /device:TPU:0, one launch (start us, length us, event | category | flops | bytes accessed | tf_op | source)
XLA Modules:
  0.0 3449.5 jit_solution(14075039186222475328)
XLA Ops:
  9.0 13.2 reshape.656
  23.9 23.2 all-gather.1
  50.9 345.3 %all-gather.16.cloned.1.call-done = bf16[32,1,548480]{2,1,0:T(2,128)(2,1)} async-done(((bf16[1,1,548480]{2,1,0:T(2,128)(2,1)}), bf16[32,1,548480]{2,1,0:T(2,128)(2,1)}) %all-gather.16.cloned.1.call-update) | async-done | bytes 35102736 | tf_op jit(solution)/shard_map/all_gather | solution.py:266
  396.2 220.1 %reduce.1 = bf16[32,548480]{1,0:T(8,128)(2,1)} reduce(bf16[32,1,548480]{2,1,0:T(2,128)(2,1)} %all-gather.16.cloned.1.call-done, bf16[]{:T(256)} %constant.289), dimensions={1}, to_apply=%all-gather.reduce_sub_computation | reduce | bytes 70205440 | tf_op jit(solution)/shard_map/all_gather | solution.py:266
  616.3 80.2 %reshape.657 = bf16[17551360]{0:T(1024)(128)(2,1)} reshape(bf16[32,548480]{1,0:T(8,128)(2,1)} %reduce.1) | data formatting | bytes 70205440
  728.4 11.4 fusion.139
  749.2 13.5 reshape.615
  762.6 13.5 slice.224
  791.7 10.9 fusion.2
  835.2 12.1 fusion.146
  875.8 25.4 all-gather.12.cloned.1.call-done
  947.8 11.3 fusion.149
  971.9 12.5 fusion.67
  1011.2 96.6 %reduce-scatter.3.cloned.1.call-done = f32[128,1024]{0,1:T(8,128)} async-done(((f32[2048,1024]{0,1:T(8,128)}), f32[128,1024]{0,1:T(8,128)}) %reduce-scatter.3.cloned.1.call-update) | async-done | bytes 524304 | tf_op jit(solution)/shard_map/reduce_scatter | solution.py:155
  1111.2 10.9 fusion.151
  1221.5 119.8 %reduce-scatter.5.cloned.1.call-done = f32[128,2048]{0,1:T(8,128)} async-done(((f32[2048,2048]{0,1:T(8,128)}), f32[128,2048]{0,1:T(8,128)}) %reduce-scatter.5.cloned.1.call-update) | async-done | bytes 1048592 | tf_op jit(solution)/shard_map/reduce_scatter | solution.py:155
  1357.7 12.3 copy.76
  1377.7 545.7 %concatenate.29 = f32[17551360]{0:T(1024)} concatenate(f32[786432]{0:T(1024)} %bitcast.185, f32[1024]{0:T(1024)} %get-tuple-element.14, f32[4096]{0:T(1024)S(1)} %bitcast.210, f32[3145728]{0:T(1024)} %bitcast.173, f32[1048576]{0:T(1024)} %bitcast.182, f32[1024]{0:T(1024)} %get-tuple-element.13, f32[4194304]{0:T(1024)} %bitcast.169, f32[4096]{0:T(1024)} %get-tuple-element.129, ...), dimensions={0} | concatenate | bytes 140410880 | tf_op jit(solution)/shard_map/concatenate | solution.py:342
  1923.4 68.2 %reshape.653 = f32[2,16,548480]{2,1,0:T(8,128)} reshape(f32[17551360]{0:T(1024)} %concatenate.29) | data formatting | bytes 140410880 | tf_op jit(solution)/shard_map/reshape | solution.py:346
  1991.6 113.0 %copy.72 = f32[2,16,548480]{2,0,1:T(2,128)} copy(f32[2,16,548480]{2,1,0:T(8,128)} %reshape.653) | data formatting | bytes 140410880 | tf_op jit(solution)/shard_map/reshape | solution.py:346
  2105.8 1137.4 %all-reduce.7.cloned.1.call-done = f32[2,16,548480]{2,0,1:T(2,128)} async-done(((f32[2,16,548480]{2,0,1:T(2,128)}), f32[2,16,548480]{2,0,1:T(2,128)}) %all-reduce.7.cloned.1.call-update) | async-done | bytes 70205456
  3251.3 110.4 %all-reduce.5.cloned.1.call-done = f32[2,1,548480]{2,0,1:T(2,128)} async-done(((f32[2,1,548480]{2,0,1:T(2,128)}), f32[2,1,548480]{2,0,1:T(2,128)}) %all-reduce.5.cloned.1.call-update) | async-done | bytes 4387856 | tf_op jit(solution)/shard_map/psum | solution.py:348
  3368.5 39.9 %all-reduce.1 = (f32[]{:T(128)}, f32[]{:T(128)}, f32[]{:T(128)}) all-reduce(f32[]{:T(128)} %get-tuple-element.30, f32[]{:T(128)} %multiply_reduce_fusion.1, f32[]{:T(128)} %get-tuple-element.29), channel_id=1, replica_groups=mesh['dp'=2,'seq'=16] {'dp','seq'}, use_global_device_ids=true, to_apply=%region_52.53 | all-reduce | flops 3 | bytes 24 | tf_op jit(solution)/shard_map/psum | solution.py:276
  3412.5 24.0 multiply_reduce_fusion
  (405 shorter events, 355.8 us)
Async XLA Ops:
  7.2 389.1 %all-gather.16.cloned.1.call-start = ((), (), s32[]{:S(2)}) async-start(), calls=%async_computation.9 | async-start | bytes 72399360 | tf_op jit(solution)/shard_map/all_gather | solution.py:266
  22.3 762.8 %all-gather.8.cloned.1.call-start = ((), (), s32[]{:S(2)}) async-start(), calls=%async_computation.2 | async-start | bytes 4456448 | tf_op jit(solution)/shard_map/all_gather | solution.py:174
  23.3 23.9 copy-start.87
  712.4 134.9 %copy-start.5 = (f32[128,1024]{1,0:T(8,128)}, f32[128,1024]{1,0:T(8,128)S(1)}, u32[]{:S(2)}) copy-start(f32[128,1024]{1,0:T(8,128)S(1)} %get-tuple-element.109) | copy-start | bytes 1572868
  728.4 100.1 %all-gather.10.cloned.1.call-start = ((), (), s32[]{:S(2)}) async-start(), calls=%async_computation.3 | async-start | bytes 4456448 | tf_op jit(solution)/shard_map/all_gather | solution.py:175
  739.8 161.4 %all-gather.12.cloned.1.call-start = ((), (), s32[]{:S(2)}) async-start(), calls=%async_computation.4 | async-start | bytes 2228224 | tf_op jit(solution)/shard_map/all_gather | solution.py:174
  746.8 44.8 %copy-start.20 = (bf16[128,1024]{0,1:T(8,128)(2,1)}, bf16[128,1024]{0,1:T(8,128)(2,1)S(1)}, u32[]{:S(2)}) copy-start(bf16[128,1024]{0,1:T(8,128)(2,1)S(1)} %copy.63) | copy-start | bytes 786436
  861.1 82.3 %all-gather.14.cloned.1.call-start = ((), (), s32[]{:S(2)}) async-start(), calls=%async_computation.5 | async-start | bytes 2228224 | tf_op jit(solution)/shard_map/all_gather | solution.py:175
  863.3 244.5 %reduce-scatter.3.cloned.1.call-start = ((), (), s32[]{:S(2)}) async-start(), calls=%async_computation.6 | async-start | bytes 8912896 | tf_op jit(solution)/shard_map/reduce_scatter | solution.py:155
  875.8 29.3 copy-start.12
  1004.0 104.9 %copy-start.14 = (bf16[512,1536]{1,0:T(8,128)(2,1)S(1)}, bf16[512,1536]{1,0:T(8,128)(2,1)}, u32[]{:S(2)}) copy-start(bf16[512,1536]{1,0:T(8,128)(2,1)} %reshape.616) | copy-start | bytes 4718596
  1004.0 337.3 %reduce-scatter.5.cloned.1.call-start = ((), (), s32[]{:S(2)}) async-start(), calls=%async_computation.7 | async-start | bytes 17825792 | tf_op jit(solution)/shard_map/reduce_scatter | solution.py:155
  1011.1 98.8 %copy-start.47 = (bf16[16,32,128]{2,1,0:T(8,128)(2,1)}, bf16[16,32,128]{2,1,0:T(8,128)(2,1)S(1)}, u32[]{:S(2)}) copy-start(bf16[16,32,128]{2,1,0:T(8,128)(2,1)S(1)} %fusion.24) | copy-start | bytes 393220
  1011.2 98.8 %copy-start.82 = (f32[128]{0:T(128)S(1)}, f32[128]{0:T(128)}, u32[]{:S(2)}) copy-start(f32[128]{0:T(128)} %get-tuple-element.44) | copy-start | bytes 1540
  1162.9 2080.3 %all-reduce.7.cloned.1.call-start = ((), (), s32[]{:S(2)}) async-start(), calls=%async_computation.10 | async-start | bytes 140410880
  1218.5 124.1 %copy-start.6 = (f32[128,1024]{1,0:T(8,128)S(1)}, f32[128,1024]{1,0:T(8,128)}, u32[]{:S(2)}) copy-start(f32[128,1024]{1,0:T(8,128)} %copy-done.5) | copy-start | bytes 1572868
  1218.5 124.1 %copy-start.54 = (f32[1024]{0:T(1024)S(1)}, f32[1024]{0:T(1024)}, u32[]{:S(2)}) copy-start(f32[1024]{0:T(1024)} %copy-done.53) | copy-start | bytes 12292
  1218.5 124.1 %copy-start.56 = (f32[1024]{0:T(1024)S(1)}, f32[1024]{0:T(1024)}, u32[]{:S(2)}) copy-start(f32[1024]{0:T(1024)} %copy-done.55) | copy-start | bytes 12292
  1218.5 124.1 %copy-start.75 = (f32[128]{0:T(128)S(1)}, f32[128]{0:T(128)}, u32[]{:S(2)}) copy-start(f32[128]{0:T(128)} %copy-done.74) | copy-start | bytes 1540
  1218.6 124.1 %copy-start.77 = (f32[128]{0:T(128)S(1)}, f32[128]{0:T(128)}, u32[]{:S(2)}) copy-start(f32[128]{0:T(128)} %copy-done.76) | copy-start | bytes 1540
  2104.6 1257.1 %all-reduce.5.cloned.1.call-start = ((), (), s32[]{:S(2)}) async-start(), calls=%async_computation.8 | async-start | bytes 8775680 | tf_op jit(solution)/shard_map/psum | solution.py:348
  3249.8 186.7 %copy-start.25 = (f32[548480]{0:T(1024)S(1)}, f32[548480]{0:T(1024)}, u32[]{:S(2)}) copy-start(f32[548480]{0:T(1024)} %param.16) | copy-start | bytes 6581764
  3412.5 24.0 copy-start.9
  3412.5 24.0 copy-start.24
  (98 other events, 594.7 us)
Sparse Core Ops, SparseCore 0:
  22.4 373.7 all-gather.15
  728.5 48.7 all-gather.7
  779.4 49.0 all-gather.9
  861.3 39.8 all-gather.11
  903.2 40.1 all-gather.13
  1004.2 103.5 reduce-scatter.2
  1163.0 178.3 reduce-scatter.4
  2104.7 1138.4 all-reduce.6
  3249.9 111.6 all-reduce.4
where the time goes:
time: 3490 us; the launch traced here: 3450 us
  waiting for transfers between devices  1850 us (53%)
  local copies, waits for them, and re-layouts  1010 us (29%)
  other arithmetic  329 us (9%)
  matrix products  173 us (5%)
  blocking collectives  63.1 us (2%)
    unnamed x10, waiting for transfers between devices  1140 us
    concatenate x1, local copies, waits for them, and re-layouts, body(): jnp.concatenate([g.reshape(-1) for g in grads] + [jnp.zeros((total_params...  546 us
    all_gather x1, waiting for transfers between devices, body(): lax.all_gather(master.astype(jnp.bfloat16), ('dp', 'seq'), axis=0, tiled=...  345 us
    all_gather x1, other arithmetic, body(): lax.all_gather(master.astype(jnp.bfloat16), ('dp', 'seq'), axis=0, tiled=...  220 us
    reduce_scatter x2, waiting for transfers between devices, attend_back(): lax.psum_scatter(jnp.concatenate([grad_keys.reshape(count, -1), grad_valu...  216 us
    reshape x2, local copies, waits for them, and re-layouts, body(): grad_flat.reshape(groups, seqs, shard)  181 us
    unnamed x235, local copies, waits for them, and re-layouts  160 us
    psum x1, waiting for transfers between devices, body(): summed = lax.psum(partial_share, 'dp')  110 us
  transfers between devices with their start and end apart: 9, of which 8 were waited for; matrix products, arithmetic and copies ran while one was open for 6% of the time, Pallas kernels for 0%

commit v1 on v0

--- a/solution.py
+++ b/solution.py
@@ -345,7 +345,8 @@
     partial_share = lax.psum_scatter(
         grad_flat.reshape(groups, seqs, shard), "seq", scatter_dimension=1, tiled=True
     )
-    summed = lax.psum(partial_share, "dp")
+    parts = lax.all_gather(partial_share, "dp", axis=0, tiled=False)
+    summed = parts.sum(axis=0)
     owned = lax.dynamic_index_in_dim(summed, lax.axis_index("dp"), 0, keepdims=False)[0]
     square_sum = jnp.sum(owned * owned)
     loss_total, square_total = lax.psum((loss_local, square_sum), ("dp", "seq"))

time: 3490 us -> 3640 us (1.043)
  other arithmetic: 329 us -> 449 us
    psum x1 -> x0, waiting for transfers between devices: 110 us -> none  [body(): summed = lax.psum(partial_share, 'dp')]
    all_gather x0 -> x1, waiting for transfers between devices: none -> 109 us  [body(): parts = lax.all_gather(partial_share, 'dp', axis=0, tiled=False)]
    all_gather x0 -> x1, other arithmetic: none -> 97 us  [body(): parts = lax.all_gather(partial_share, 'dp', axis=0, tiled=False)]
where the time goes in v1:
time: 3640 us; the launch traced here: 3590 us
  waiting for transfers between devices  1850 us (51%)
  local copies, waits for them, and re-layouts  1030 us (28%)
  other arithmetic  449 us (12%)
  matrix products  173 us (5%)
  blocking collectives  62.8 us (2%)
    unnamed x10, waiting for transfers between devices  1140 us
    concatenate x1, local copies, waits for them, and re-layouts, body(): jnp.concatenate([g.reshape(-1) for g in grads] + [jnp.zeros((total_params...  546 us
    all_gather x1, waiting for transfers between devices, body(): lax.all_gather(master.astype(jnp.bfloat16), ('dp', 'seq'), axis=0, tiled=...  345 us
    all_gather x1, other arithmetic, body(): lax.all_gather(master.astype(jnp.bfloat16), ('dp', 'seq'), axis=0, tiled=...  220 us
    reduce_scatter x2, waiting for transfers between devices, attend_back(): lax.psum_scatter(jnp.concatenate([grad_keys.reshape(count, -1), grad_valu...  217 us
    reshape x2, local copies, waits for them, and re-layouts, body(): grad_flat.reshape(groups, seqs, shard)  181 us
    unnamed x235, local copies, waits for them, and re-layouts  157 us
    all_gather x1, waiting for transfers between devices, body(): parts = lax.all_gather(partial_share, 'dp', axis=0, tiled=False)  109 us
  transfers between devices with their start and end apart: 9, of which 8 were waited for; matrix products, arithmetic and copies ran while one was open for 6% of the time, Pallas kernels for 0%

profile of v1, /device:TPU:0, one launch (start us, length us, event | category | flops | bytes accessed | tf_op | source)
XLA Modules:
  0.0 3592.4 jit_solution(932817037744513934)
XLA Ops:
  9.0 13.2 reshape.661
  23.9 23.2 all-gather.2
  51.0 345.3 %all-gather.20.cloned.1.call-done = bf16[32,1,548480]{2,1,0:T(2,128)(2,1)} async-done(((bf16[1,1,548480]{2,1,0:T(2,128)(2,1)}), bf16[32,1,548480]{2,1,0:T(2,128)(2,1)}) %all-gather.20.cloned.1.call-update) | async-done | bytes 35102736 | tf_op jit(solution)/shard_map/all_gather | solution.py:266
  396.2 220.1 %reduce.3 = bf16[32,548480]{1,0:T(8,128)(2,1)} reduce(bf16[32,1,548480]{2,1,0:T(2,128)(2,1)} %all-gather.20.cloned.1.call-done, bf16[]{:T(256)} %constant.289), dimensions={1}, to_apply=%all-gather.1.reduce_sub_computation | reduce | bytes 70205440 | tf_op jit(solution)/shard_map/all_gather | solution.py:266
  616.3 80.1 %reshape.662 = bf16[17551360]{0:T(1024)(128)(2,1)} reshape(bf16[32,548480]{1,0:T(8,128)(2,1)} %reduce.3) | data formatting | bytes 70205440
  728.2 11.4 fusion.139
  748.9 13.5 reshape.618
  762.4 13.5 slice.224
  835.0 12.1 fusion.146
  875.5 25.5 all-gather.14.cloned.1.call-done
  971.7 12.5 fusion.67
  1010.7 96.6 %reduce-scatter.3.cloned.1.call-done = f32[128,1024]{0,1:T(8,128)} async-done(((f32[2048,1024]{0,1:T(8,128)}), f32[128,1024]{0,1:T(8,128)}) %reduce-scatter.3.cloned.1.call-update) | async-done | bytes 524304 | tf_op jit(solution)/shard_map/reduce_scatter | solution.py:155
  1220.8 120.0 %reduce-scatter.5.cloned.1.call-done = f32[128,2048]{0,1:T(8,128)} async-done(((f32[2048,2048]{0,1:T(8,128)}), f32[128,2048]{0,1:T(8,128)}) %reduce-scatter.5.cloned.1.call-update) | async-done | bytes 1048592 | tf_op jit(solution)/shard_map/reduce_scatter | solution.py:155
  1357.1 12.2 copy.80
  1377.0 545.6 %concatenate.29 = f32[17551360]{0:T(1024)} concatenate(f32[786432]{0:T(1024)} %bitcast.185, f32[1024]{0:T(1024)} %get-tuple-element.14, f32[4096]{0:T(1024)S(1)} %bitcast.210, f32[3145728]{0:T(1024)} %bitcast.173, f32[1048576]{0:T(1024)} %bitcast.182, f32[1024]{0:T(1024)} %get-tuple-element.13, f32[4194304]{0:T(1024)} %bitcast.169, f32[4096]{0:T(1024)} %get-tuple-element.129, ...), dimensions={0} | concatenate | bytes 140410880 | tf_op jit(solution)/shard_map/concatenate | solution.py:342
  1922.7 67.9 %reshape.656 = f32[2,16,548480]{2,1,0:T(8,128)} reshape(f32[17551360]{0:T(1024)} %concatenate.29) | data formatting | bytes 140410880 | tf_op jit(solution)/shard_map/reshape | solution.py:346
  1990.6 113.0 %copy.74 = f32[2,16,548480]{2,0,1:T(2,128)} copy(f32[2,16,548480]{2,1,0:T(8,128)} %reshape.656) | data formatting | bytes 140410880 | tf_op jit(solution)/shard_map/reshape | solution.py:346
  2104.8 1137.3 %all-reduce.4.cloned.1.call-done = f32[2,16,548480]{2,0,1:T(2,128)} async-done(((f32[2,16,548480]{2,0,1:T(2,128)}), f32[2,16,548480]{2,0,1:T(2,128)}) %all-reduce.4.cloned.1.call-update) | async-done | bytes 70205456
  3255.4 109.2 %all-gather.18.cloned.1.call-done = f32[4,1,548480]{2,1,0:T(1,128)} async-done(((f32[2,1,548480]{2,1,0:T(1,128)}), f32[4,1,548480]{2,1,0:T(1,128)}) %all-gather.18.cloned.1.call-update) | async-done | bytes 8775696 | tf_op jit(solution)/shard_map/all_gather | solution.py:348
  3364.6 97.0 %reduce.4 = f32[4,548480]{1,0:T(4,128)} reduce(f32[4,1,548480]{2,1,0:T(1,128)} %all-gather.18.cloned.1.call-done, f32[]{:T(128)} %constant.290), dimensions={1}, to_apply=%all-gather.reduce_sub_computation | reduce | bytes 17551364 | tf_op jit(solution)/shard_map/all_gather | solution.py:348
  3461.6 20.1 reshape.659
  3481.7 23.2 reduce.2
  3511.7 39.6 %all-reduce.1 = (f32[]{:T(128)}, f32[]{:T(128)}, f32[]{:T(128)}) all-reduce(f32[]{:T(128)} %get-tuple-element.30, f32[]{:T(128)} %multiply_reduce_fusion.1, f32[]{:T(128)} %get-tuple-element.29), channel_id=1, replica_groups=mesh['dp'=2,'seq'=16] {'dp','seq'}, use_global_device_ids=true, to_apply=%region_52.53 | all-reduce | flops 3 | bytes 24 | tf_op jit(solution)/shard_map/psum | solution.py:276
  3555.5 24.0 multiply_reduce_fusion
  (409 shorter events, 393.6 us)
Async XLA Ops:
  7.2 389.1 %all-gather.20.cloned.1.call-start = ((), (), s32[]{:S(2)}) async-start(), calls=%async_computation.9 | async-start | bytes 72399360 | tf_op jit(solution)/shard_map/all_gather | solution.py:266
  22.3 762.6 %all-gather.10.cloned.1.call-start = ((), (), s32[]{:S(2)}) async-start(), calls=%async_computation.2 | async-start | bytes 4456448 | tf_op jit(solution)/shard_map/all_gather | solution.py:174
  23.3 23.9 copy-start.87
  712.2 135.0 %copy-start.5 = (f32[128,1024]{1,0:T(8,128)}, f32[128,1024]{1,0:T(8,128)S(1)}, u32[]{:S(2)}) copy-start(f32[128,1024]{1,0:T(8,128)S(1)} %get-tuple-element.109) | copy-start | bytes 1572868
  728.2 100.1 %all-gather.12.cloned.1.call-start = ((), (), s32[]{:S(2)}) async-start(), calls=%async_computation.3 | async-start | bytes 4456448 | tf_op jit(solution)/shard_map/all_gather | solution.py:175
  739.6 161.3 %all-gather.14.cloned.1.call-start = ((), (), s32[]{:S(2)}) async-start(), calls=%async_computation.4 | async-start | bytes 2228224 | tf_op jit(solution)/shard_map/all_gather | solution.py:174
  746.6 44.7 %copy-start.20 = (bf16[128,1024]{0,1:T(8,128)(2,1)}, bf16[128,1024]{0,1:T(8,128)(2,1)S(1)}, u32[]{:S(2)}) copy-start(bf16[128,1024]{0,1:T(8,128)(2,1)S(1)} %copy.65) | copy-start | bytes 786436
  860.9 82.3 %all-gather.16.cloned.1.call-start = ((), (), s32[]{:S(2)}) async-start(), calls=%async_computation.5 | async-start | bytes 2228224 | tf_op jit(solution)/shard_map/all_gather | solution.py:175
  863.0 244.3 %reduce-scatter.3.cloned.1.call-start = ((), (), s32[]{:S(2)}) async-start(), calls=%async_computation.6 | async-start | bytes 8912896 | tf_op jit(solution)/shard_map/reduce_scatter | solution.py:155
  875.5 29.4 copy-start.12
  1003.6 104.9 %copy-start.14 = (bf16[512,1536]{1,0:T(8,128)(2,1)S(1)}, bf16[512,1536]{1,0:T(8,128)(2,1)}, u32[]{:S(2)}) copy-start(bf16[512,1536]{1,0:T(8,128)(2,1)} %reshape.619) | copy-start | bytes 4718596
  1003.6 337.3 %reduce-scatter.5.cloned.1.call-start = ((), (), s32[]{:S(2)}) async-start(), calls=%async_computation.7 | async-start | bytes 17825792 | tf_op jit(solution)/shard_map/reduce_scatter | solution.py:155
  1010.7 98.8 %copy-start.47 = (bf16[16,32,128]{2,1,0:T(8,128)(2,1)}, bf16[16,32,128]{2,1,0:T(8,128)(2,1)S(1)}, u32[]{:S(2)}) copy-start(bf16[16,32,128]{2,1,0:T(8,128)(2,1)S(1)} %fusion.24) | copy-start | bytes 393220
  1010.7 98.8 %copy-start.82 = (f32[128]{0:T(128)S(1)}, f32[128]{0:T(128)}, u32[]{:S(2)}) copy-start(f32[128]{0:T(128)} %get-tuple-element.44) | copy-start | bytes 1540
  1162.4 2079.8 %all-reduce.4.cloned.1.call-start = ((), (), s32[]{:S(2)}) async-start(), calls=%async_computation.10 | async-start | bytes 140410880
  1217.8 124.3 %copy-start.6 = (f32[128,1024]{1,0:T(8,128)S(1)}, f32[128,1024]{1,0:T(8,128)}, u32[]{:S(2)}) copy-start(f32[128,1024]{1,0:T(8,128)} %copy-done.5) | copy-start | bytes 1572868
  1217.8 124.3 %copy-start.54 = (f32[1024]{0:T(1024)S(1)}, f32[1024]{0:T(1024)}, u32[]{:S(2)}) copy-start(f32[1024]{0:T(1024)} %copy-done.53) | copy-start | bytes 12292
  1217.8 124.3 %copy-start.56 = (f32[1024]{0:T(1024)S(1)}, f32[1024]{0:T(1024)}, u32[]{:S(2)}) copy-start(f32[1024]{0:T(1024)} %copy-done.55) | copy-start | bytes 12292
  1217.8 124.3 %copy-start.75 = (f32[128]{0:T(128)S(1)}, f32[128]{0:T(128)}, u32[]{:S(2)}) copy-start(f32[128]{0:T(128)} %copy-done.74) | copy-start | bytes 1540
  1217.8 124.3 %copy-start.77 = (f32[128]{0:T(128)S(1)}, f32[128]{0:T(128)}, u32[]{:S(2)}) copy-start(f32[128]{0:T(128)} %copy-done.76) | copy-start | bytes 1540
  2103.6 1261.0 %all-gather.18.cloned.1.call-start = ((), (), s32[]{:S(2)}) async-start(), calls=%async_computation.8 | async-start | bytes 13163520 | tf_op jit(solution)/shard_map/all_gather | solution.py:348
  3481.7 97.7 %copy-start.25 = (f32[548480]{0:T(1024)S(1)}, f32[548480]{0:T(1024)}, u32[]{:S(2)}) copy-start(f32[548480]{0:T(1024)} %param.16) | copy-start | bytes 6581764
  3555.4 24.0 copy-start.9
  3555.4 24.0 copy-start.24
  (98 other events, 593.4 us)
Sparse Core Ops, SparseCore 0:
  22.4 373.7 all-gather.19
  728.3 48.7 all-gather.9
  779.2 49.0 all-gather.11
  861.0 39.8 all-gather.13
  902.9 40.1 all-gather.15
  1003.7 103.5 reduce-scatter.2
  1162.5 178.2 reduce-scatter.4
  2103.8 1138.3 all-reduce.3
  3254.2 110.3 all-gather.17
